TPU v7x, 256 devices: a whole 4x4x8 slice. The times are simulated.
256 devices in a mesh: dp: 2 (over z_hi), context: 8 (over y, core), tensor: 16 (over z_lo, x).
Axes of the slice: x: 4, y: 4, z: 8 (z_hi: 2, z_lo: 4; z = z_hi * 4 + z_lo), core: 2. Of those that a mesh axis runs over, the one named last changes fastest.
Arguments:
- tokens: bfloat16 [2, 4096, 5376], P('dp', ('context', 'tensor')), may hold values from -48 to 48
- output_gradient: bfloat16 [2, 4096, 5376], P('dp', ('context', 'tensor')), may hold values from -48 to 48
- document_index: int32 [2, 4096], P('dp'), may hold values from 0 to 3, never falling along the last dimension, each value on 1 to 2048 neighbouring positions
- query_weight: bfloat16 [5376, 4096], P(None, 'tensor'), may hold values from -1 to 1
- key_value_weight: bfloat16 [2, 5376, 2048], P(None, None, 'tensor'), may hold values from -1 to 1
- output_weight: bfloat16 [4096, 5376], P('tensor'), may hold values from -0.09375 to 0.09375
- adapter_down_projections: bfloat16 [3, 16, 5376], replicated, may hold values from -0.078125 to 0.078125
- adapter_up_query: bfloat16 [16, 4096], P(None, 'tensor'), may hold values from -0.29882812 to 0.29882812
- adapter_up_key_value: bfloat16 [2, 16, 2048], P(None, None, 'tensor'), may hold values from -0.29882812 to 0.29882812
- adapter_down_output: bfloat16 [16, 4096], P(None, 'tensor'), may hold values from -0.09375 to 0.09375
- adapter_up_output: bfloat16 [16, 5376], replicated, may hold values from -0.29882812 to 0.29882812
Outputs:
- grad_input: bfloat16 [2, 4096, 5376], P('dp', ('context', 'tensor'))
- grad_down_qkv: float32 [3, 16, 5376], replicated
- query_up_gradient: float32 [16, 4096], P(None, 'tensor')
- grad_up_keyvalue: float32 [2, 16, 2048], P(None, None, 'tensor')
- grad_down_out: float32 [16, 4096], P(None, 'tensor')
- output_up_gradient: float32 [16, 5376], replicated
Inputs may be any that keep to these rules, and one draw needn't show every extreme that they name: `document_index`: ids never fall along a sequence; each document holds 1 to half of 4096 tokens, and one holds exactly that many.
All inputs are finite; a program needn't handle non-finite values.
Results may differ from a plain program's by a relative error of at most 0.03.
Values may be sent and summed in bfloat16 or wider, within the bound.
No kernel may reach another device: no remote copies, remote signals or barrier semaphores. Data moves between devices by JAX's collectives and lax.ppermute only.
A program may use at most 128 MiB of HBM per device.

v0:
```python
import jax
import jax.numpy as jnp
from jax import lax
from jax.sharding import PartitionSpec as P

HEAD_SIZE = 128
WINDOW = 1024
adapter_scale = 2.0
attn_scale = 168.0 ** (-0.5)
rope_base = 10000.0


def passed_along(block, axis, distance):
    devices = range(lax.axis_size(axis))
    route = [(i - distance, i) for i in devices if i - distance in devices]
    return lax.ppermute(block, axis, route)


def rope_tables(positions, head_width):
    half_width = head_width // 2
    inverse = rope_base ** (-(jnp.arange(half_width, dtype=jnp.float32) * 2.0 / head_width))
    angle = positions[:, None] * inverse[None, :]
    return (jnp.cos(angle), jnp.sin(angle))


def apply_rotation(vectors, cosine_table, sine_values):
    half_width = vectors.shape[-1] // 2
    front_half = vectors[..., :half_width]
    back_half = vectors[..., half_width:]
    cosine_table = cosine_table[:, None, :]
    sine_values = sine_values[:, None, :]
    return jnp.concatenate(
        [
            front_half * cosine_table - back_half * sine_values,
            back_half * cosine_table + front_half * sine_values,
        ],
        -1,
    )


def undo_rotation(grads, cosine_table, sine_values):
    half_width = grads.shape[-1] // 2
    front_half = grads[..., :half_width]
    back_half = grads[..., half_width:]
    cosine_table = cosine_table[:, None, :]
    sine_values = sine_values[:, None, :]
    return jnp.concatenate(
        [
            front_half * cosine_table + back_half * sine_values,
            back_half * cosine_table - front_half * sine_values,
        ],
        -1,
    )


def band_block(queries, key_rows, value_rows, attention_output_gradient, allowed):
    row_count, heads_q, head_width = queries.shape
    heads_kv = key_rows.shape[1]
    group_size = heads_q // heads_kv
    query_groups = queries.reshape(row_count, heads_kv, group_size, head_width)
    grad_groups = attention_output_gradient.reshape(row_count, heads_kv, group_size, head_width)
    scores = (
        jnp.einsum("chgd,khd->hgck", query_groups, key_rows, preferred_element_type=jnp.float32)
        * attn_scale
    )
    scores = jnp.where(allowed[None, None], scores, -1e30)
    row_max = jnp.max(scores, -1, keepdims=True)
    exponent = jnp.exp(scores - row_max)
    weights = exponent / jnp.sum(exponent, -1, keepdims=True)
    weights_low = weights.astype(jnp.bfloat16)
    attention_output = jnp.einsum(
        "hgck,khd->chgd", weights_low, value_rows, preferred_element_type=jnp.float32
    ).astype(jnp.bfloat16)
    grad_weights = jnp.einsum(
        "chgd,khd->hgck", grad_groups, value_rows, preferred_element_type=jnp.float32
    )
    row_dot = jnp.einsum(
        "chgd,chgd->hgc", grad_groups.astype(jnp.float32), attention_output.astype(jnp.float32)
    )
    grad_scores = (weights * (grad_weights - row_dot[..., None]) * attn_scale).astype(jnp.bfloat16)
    query_gradient = jnp.einsum(
        "hgck,khd->chgd", grad_scores, key_rows, preferred_element_type=jnp.float32
    )
    key_gradient = jnp.einsum(
        "hgck,chgd->khd", grad_scores, query_groups, preferred_element_type=jnp.float32
    )
    value_gradient = jnp.einsum(
        "hgck,chgd->khd", weights_low, grad_groups, preferred_element_type=jnp.float32
    )
    return (
        attention_output.reshape(row_count, heads_q, head_width),
        query_gradient.reshape(row_count, heads_q, head_width),
        key_gradient,
        value_gradient,
    )


def local(
    tokens,
    output_gradient,
    document_index,
    query_weight,
    key_value_weight,
    output_weight,
    adapter_down_projections,
    adapter_up_query,
    adapter_up_key_value,
    adapter_down_output,
    adapter_up_output,
):
    tensor_size = lax.axis_size("tensor")
    context_at = lax.axis_index("context")
    local_count = tokens.shape[1]
    model_width_size = tokens.shape[2]
    shard_len = local_count * tensor_size
    halo_count = (WINDOW - 1) // shard_len + 1
    rank_width_size = adapter_down_projections.shape[1]
    heads_q = query_weight.shape[1] // HEAD_SIZE
    heads_kv = key_value_weight.shape[2] // HEAD_SIZE
    gathered, incoming_gradient = (
        lax.all_gather(tokens[0], "tensor", axis=0, tiled=True),
        lax.all_gather(output_gradient[0], "tensor", axis=0, tiled=True),
    )
    down_factors_all = adapter_down_projections.reshape(3 * rank_width_size, model_width_size)
    adapted = jnp.einsum(
        "ja,ma->jm", gathered, down_factors_all, preferred_element_type=jnp.float32
    ).astype(jnp.bfloat16)
    adapted_query = adapted[:, :rank_width_size]
    adapted_key = adapted[:, rank_width_size : 2 * rank_width_size]
    adapted_value = adapted[:, 2 * rank_width_size :]
    query_linear = jnp.dot(
        gathered, query_weight, preferred_element_type=jnp.float32
    ) + adapter_scale * jnp.dot(adapted_query, adapter_up_query, preferred_element_type=jnp.float32)
    key_linear = jnp.dot(
        gathered, key_value_weight[0], preferred_element_type=jnp.float32
    ) + adapter_scale * jnp.dot(
        adapted_key, adapter_up_key_value[0], preferred_element_type=jnp.float32
    )
    value_linear = jnp.dot(
        gathered, key_value_weight[1], preferred_element_type=jnp.float32
    ) + adapter_scale * jnp.dot(
        adapted_value, adapter_up_key_value[1], preferred_element_type=jnp.float32
    )
    positions = (context_at * shard_len + jnp.arange(shard_len, dtype=jnp.int32)).astype(
        jnp.float32
    )
    cosine_table, sine_values = rope_tables(positions, HEAD_SIZE)
    queries = apply_rotation(
        query_linear.reshape(shard_len, heads_q, HEAD_SIZE), cosine_table, sine_values
    ).astype(jnp.bfloat16)
    key_local = apply_rotation(
        key_linear.reshape(shard_len, heads_kv, HEAD_SIZE), cosine_table, sine_values
    ).astype(jnp.bfloat16)
    value_local = value_linear.reshape(shard_len, heads_kv, HEAD_SIZE).astype(jnp.bfloat16)
    pair_local = jnp.stack([key_local, value_local], 0)
    earlier = [
        passed_along(pair_local, "context", distance) for distance in range(halo_count, 0, -1)
    ]
    pairs = jnp.concatenate(earlier + [pair_local], 1)
    segment_row = document_index[0]
    segment_pad = jnp.concatenate(
        [jnp.full((halo_count * shard_len,), -1, jnp.int32), segment_row], 0
    )
    key_seg = lax.dynamic_slice_in_dim(
        segment_pad, context_at * shard_len, (halo_count + 1) * shard_len, 0
    )
    query_seg = lax.dynamic_slice_in_dim(segment_row, context_at * shard_len, shard_len, 0)
    query_pos = context_at * shard_len + jnp.arange(shard_len, dtype=jnp.int32)
    key_pos = (context_at - halo_count) * shard_len + jnp.arange(
        (halo_count + 1) * shard_len, dtype=jnp.int32
    )
    offset = query_pos[:, None] - key_pos[None, :]
    allowed = (
        (key_pos >= 0)[None, :]
        & (offset >= 0)
        & (offset < WINDOW)
        & (query_seg[:, None] == key_seg[None, :])
    )
    up_gradient = (
        adapter_scale
        * jnp.einsum(
            "ja,ma->jm", incoming_gradient, adapter_up_output, preferred_element_type=jnp.float32
        )
    ).astype(jnp.bfloat16)
    attention_output_gradient = (
        jnp.einsum(
            "td,hd->th", incoming_gradient, output_weight, preferred_element_type=jnp.float32
        )
        + jnp.dot(up_gradient, adapter_down_output, preferred_element_type=jnp.float32)
    ).astype(jnp.bfloat16)
    attention_output, grad_query_rot, grad_keys_all, grad_values_all = band_block(
        queries,
        pairs[0],
        pairs[1],
        attention_output_gradient.reshape(shard_len, heads_q, HEAD_SIZE),
        allowed,
    )
    grad_pairs = jnp.stack([grad_keys_all, grad_values_all], 0)

    def share_for(distance):
        return lax.slice_in_dim(
            grad_pairs,
            (halo_count - distance) * shard_len,
            (halo_count - distance + 1) * shard_len,
            axis=1,
        )

    combined = share_for(0)
    for distance in range(1, halo_count + 1):
        combined = combined + passed_along(
            share_for(distance).astype(jnp.bfloat16), "context", -distance
        ).astype(jnp.float32)
    attention_output_flat = attention_output.reshape(shard_len, heads_q * HEAD_SIZE)
    query_gradient = (
        undo_rotation(grad_query_rot, cosine_table, sine_values)
        .reshape(shard_len, heads_q * HEAD_SIZE)
        .astype(jnp.bfloat16)
    )
    key_gradient = (
        undo_rotation(combined[0], cosine_table, sine_values)
        .reshape(shard_len, heads_kv * HEAD_SIZE)
        .astype(jnp.bfloat16)
    )
    value_gradient = combined[1].reshape(shard_len, heads_kv * HEAD_SIZE).astype(jnp.bfloat16)
    query_hidden = (
        adapter_scale
        * jnp.einsum(
            "kn,pn->kp", query_gradient, adapter_up_query, preferred_element_type=jnp.float32
        )
    ).astype(jnp.bfloat16)
    key_hidden = (
        adapter_scale
        * jnp.einsum(
            "kn,pn->kp", key_gradient, adapter_up_key_value[0], preferred_element_type=jnp.float32
        )
    ).astype(jnp.bfloat16)
    value_hidden = (
        adapter_scale
        * jnp.einsum(
            "kn,pn->kp", value_gradient, adapter_up_key_value[1], preferred_element_type=jnp.float32
        )
    ).astype(jnp.bfloat16)
    hidden_all = jnp.concatenate([query_hidden, key_hidden, value_hidden], 1)
    grad_down_part = jnp.einsum(
        "tr,td->rd", hidden_all, gathered, preferred_element_type=jnp.float32
    ).reshape(3, rank_width_size, model_width_size)
    query_up_gradient_piece = adapter_scale * jnp.einsum(
        "tr,th->rh", adapted_query, query_gradient, preferred_element_type=jnp.float32
    )
    grad_up_kv_part = jnp.stack(
        [
            adapter_scale
            * jnp.einsum(
                "tr,th->rh", adapted_key, key_gradient, preferred_element_type=jnp.float32
            ),
            adapter_scale
            * jnp.einsum(
                "tr,th->rh", adapted_value, value_gradient, preferred_element_type=jnp.float32
            ),
        ],
        0,
    )
    grad_down_out_part = jnp.einsum(
        "tr,th->rh", up_gradient, attention_output_flat, preferred_element_type=jnp.float32
    )
    factor_part = jnp.einsum(
        "kn,pn->kp", attention_output_flat, adapter_down_output, preferred_element_type=jnp.float32
    )
    factor_value = lax.psum(factor_part.astype(jnp.bfloat16), "tensor")
    output_up_gradient_piece = adapter_scale * jnp.einsum(
        "tr,td->rd", factor_value, incoming_gradient, preferred_element_type=jnp.float32
    )
    grad_down_qkv = lax.psum(grad_down_part, ("dp", "context", "tensor"))
    query_up_gradient, grad_up_keyvalue, grad_down_out, output_up_gradient = (
        lax.psum(query_up_gradient_piece.astype(jnp.bfloat16), ("dp", "context")).astype(
            jnp.float32
        ),
        lax.psum(grad_up_kv_part.astype(jnp.bfloat16), ("dp", "context")).astype(jnp.float32),
        lax.psum(grad_down_out_part.astype(jnp.bfloat16), ("dp", "context")).astype(jnp.float32),
        lax.psum(output_up_gradient_piece.astype(jnp.bfloat16), ("dp", "context")).astype(
            jnp.float32
        ),
    )
    term = jnp.einsum("th,dh->td", query_gradient, query_weight, preferred_element_type=jnp.float32)
    term = term + jnp.einsum(
        "th,dh->td", key_gradient, key_value_weight[0], preferred_element_type=jnp.float32
    )
    term = term + jnp.einsum(
        "th,dh->td", value_gradient, key_value_weight[1], preferred_element_type=jnp.float32
    )
    full_sum = lax.psum(
        (term + jnp.dot(hidden_all, down_factors_all, preferred_element_type=jnp.float32)).astype(
            jnp.bfloat16
        ),
        "tensor",
    ).astype(jnp.float32)
    mine = lax.dynamic_slice_in_dim(
        full_sum, lax.axis_index("tensor") * local_count, local_count, 0
    )
    grad_input = mine.astype(jnp.bfloat16)[None]
    return (
        grad_input,
        grad_down_qkv,
        query_up_gradient,
        grad_up_keyvalue,
        grad_down_out,
        output_up_gradient,
    )


def solution(mesh):
    in_specs = (
        P("dp", ("context", "tensor"), None),
        P("dp", ("context", "tensor"), None),
        P("dp", None),
        P(None, "tensor"),
        P(None, None, "tensor"),
        P("tensor", None),
        P(),
        P(None, "tensor"),
        P(None, None, "tensor"),
        P(None, "tensor"),
        P(),
    )
    out_specs = (
        P("dp", ("context", "tensor"), None),
        P(),
        P(None, "tensor"),
        P(None, None, "tensor"),
        P(None, "tensor"),
        P(),
    )
    return jax.shard_map(local, mesh=mesh, in_specs=in_specs, out_specs=out_specs, check_vma=False)
```

profile of v0, /device:TPU:2, one launch (start us, length us, event | category | flops | bytes accessed | tf_op | source)
XLA Modules:
  0.0 926.9 jit_solution(11296037939888309069)
XLA Ops:
  10.3 1.8 multiply_cosine_fusion
  13.8 86.9 %all-gather.5.cloned.1.call-done = bf16[1,512,5376]{2,1,0:T(8,128)(2,1)} async-done(((bf16[1,32,5376]{2,1,0:T(8,128)(2,1)}), bf16[1,512,5376]{2,1,0:T(8,128)(2,1)}) %all-gather.5.cloned.1.call-update) | async-done | bytes 5505040 | tf_op jit(solution)/shard_map/all_gather | solution.py:121
  100.6 4.5 fusion.55
  105.2 3.5 fusion.15
  109.0 2.0 fusion.19
  112.5 2.0 collective-permute-start.1
  114.5 4.0 collective-permute-start
  121.4 1.9 copy.65
  123.3 2.0 copy.64
  125.3 67.7 %all-gather.7.cloned.1.call-done = bf16[1,512,5376]{2,1,0:T(8,128)(2,1)} async-done(((bf16[1,32,5376]{2,1,0:T(8,128)(2,1)}), bf16[1,512,5376]{2,1,0:T(8,128)(2,1)}) %all-gather.7.cloned.1.call-update) | async-done | bytes 5505040 | tf_op jit(solution)/shard_map/all_gather | solution.py:122
  193.0 4.2 fusion.61
  197.3 3.5 fusion.9
  205.6 2.2 fusion.75
  207.8 3.3 fusion.31
  211.1 2.8 fusion.22
  214.0 2.2 convolution_bitcast_fusion.1
  218.5 75.9 %psum.54 = bf16[512,16]{1,0:T(8,128)(2,1)} all-reduce(bf16[512,16]{1,0:T(8,128)(2,1)} %convolution_convert_fusion), channel_id=1, replica_groups=mesh['dp'=2,'context'=8,'tensor'=16] {'tensor'}, use_global_device_ids=true, to_apply=%region_7.8 | all-reduce | flops 8192 | bytes 32768 | tf_op jit(solution)/shard_map/psum | solution.py:269
  294.3 4.2 fusion
  305.7 1.8 copy.40
  308.6 6.3 collective-permute-done.3
  317.0 7.3 fusion.35
  325.1 5.6 fusion.38
  330.7 5.7 fusion.99
  336.4 14.6 %add_convert_fusion = bf16[512,5376]{1,0:T(8,128)(2,1)} fusion(f32[512,5376]{1,0:T(8,128)} %fusion.99, f32[512,5376]{1,0:T(8,128)} %fusion.35, f32[512,5376]{1,0:T(8,128)} %fusion.38, bf16[512,256]{0,1:T(8,128)(2,1)S(1)} %bitcast.198, bf16[5376,256]{1,0:T(8,128)(2,1)S(1)} %copy-done), kind=kOutput, calls=%fused_computation | convolution fusion | flops 1420296192 | bytes 41549824 | tf_op jit(solution)/shard_map/th,dh->td/dot_general | solution.py:284
  351.0 1.8 convolution_convert_fusion.1
  354.3 114.1 %all-reduce.10.cloned.1.call-done = bf16[16,5376]{1,0:T(8,128)(2,1)} async-done(((bf16[16,5376]{1,0:T(8,128)(2,1)}), bf16[16,5376]{1,0:T(8,128)(2,1)}) %all-reduce.10.cloned.1.call-update) | async-done | bytes 172048 | tf_op jit(solution)/shard_map/psum | solution.py:280
  472.0 90.5 %all-reduce.1 = (bf16[16,256]{1,0:T(8,128)(2,1)S(1)}, bf16[2,16,128]{2,1,0:T(8,128)(2,1)S(1)}, bf16[16,256]{1,0:T(8,128)(2,1)S(1)}) all-reduce(bf16[16,256]{1,0:T(8,128)(2,1)} %fusion.67, bf16[2,16,128]{2,1,0:T(8,128)(2,1)S(1)} %pad_maximum_fusion.12, ...), channel_id=1, replica_groups=mesh['dp'=2,'context'=8,'tensor'=16] {'dp','context'}, use_global_device_ids=true, to_apply=%region_4.5 | all-reduce | flops 12288 | bytes 49152 | tf_op jit(solution)/shard_map/psum | solution.py:275
  564.4 4.7 fusion.11
  569.1 85.8 %all-reduce.6.cloned.1.call-done = bf16[512,5376]{1,0:T(8,128)(2,1)} async-done(((bf16[512,5376]{1,0:T(8,128)(2,1)}), bf16[512,5376]{1,0:T(8,128)(2,1)}) %all-reduce.6.cloned.1.call-update) | async-done | bytes 5505040 | tf_op jit(solution)/shard_map/psum | solution.py:291
  654.9 1.7 fusion.77
  656.6 261.6 %all-reduce.8.cloned.1.call-done = f32[3,16,5376]{2,1,0:T(8,128)} async-done(((f32[3,16,5376]{2,1,0:T(8,128)}), f32[3,16,5376]{2,1,0:T(8,128)}) %all-reduce.8.cloned.1.call-update) | async-done | bytes 1032208 | tf_op jit(solution)/shard_map/psum | solution.py:273
  918.1 2.2 copy.69
  (122 shorter events, 34.3 us)
Async XLA Ops:
  7.2 111.4 %copy-start = (bf16[5376,256]{1,0:T(8,128)(2,1)S(1)}, bf16[5376,256]{1,0:T(8,128)(2,1)}, u32[]{:S(2)}) copy-start(bf16[5376,256]{1,0:T(8,128)(2,1)} %param.14) | copy-start | bytes 8257540
  7.2 93.5 %all-gather.5.cloned.1.call-start = ((), (), s32[]{:S(2)}) async-start(), calls=%async_computation.3 | async-start | bytes 5849088 | tf_op jit(solution)/shard_map/all_gather | solution.py:121
  7.9 185.1 %all-gather.7.cloned.1.call-start = ((), (), s32[]{:S(2)}) async-start(), calls=%async_computation.4 | async-start | bytes 5849088 | tf_op jit(solution)/shard_map/all_gather | solution.py:122
  8.7 459.8 %all-reduce.10.cloned.1.call-start = ((), (), s32[]{:S(2)}) async-start(), calls=%async_computation.2 | async-start | bytes 344064 | tf_op jit(solution)/shard_map/psum | solution.py:280
  8.7 102.4 %copy-start.32 = (f32[64]{0:T(128)}, f32[64]{0:T(128)S(1)}, u32[]{:S(2)}) copy-start(f32[64]{0:T(128)S(1)} %negate_power_fusion) | copy-start | bytes 772
  8.8 102.4 %copy-start.26 = (f32[512]{0:T(512)}, f32[512]{0:T(512)S(1)}, u32[]{:S(2)}) copy-start(f32[512]{0:T(512)S(1)} %fusion.114) | copy-start | bytes 6148
  100.6 4.5 copy-start.1
  105.2 15.1 %copy-start.20 = (bf16[512,48]{0,1:T(8,128)(2,1)}, bf16[512,48]{0,1:T(8,128)(2,1)S(1)}, u32[]{:S(2)}) copy-start(bf16[512,48]{0,1:T(8,128)(2,1)S(1)} %fusion.55) | copy-start | bytes 147460
  111.2 9.1 copy-start.29
  112.5 88.8 %collective-permute-start.1 = (bf16[2,512,1,128]{1,3,2,0:T(8,128)(2,1)}, bf16[2,512,1,128]{1,3,2,0:T(8,128)(2,1)}, u32[]{:S(2)}, u32[]{:S(2)}) collective-permute-start(bf16[2,512,1,128]{1,3,2,0:T(8,128)(2,1)} %pad_maximum_fusion.1), channel_id=1, source_target_pairs={{0,16},{16,32},{32,48},{48,64},{64,80},{80,96},{96,112},{1,17},{17... | collective-permute-start | bytes 786440 | tf_op jit(solution)/shard_map/ppermute | solution.py:16
  114.5 86.8 %collective-permute-start = (bf16[2,512,1,128]{1,3,2,0:T(8,128)(2,1)}, bf16[2,512,1,128]{1,3,2,0:T(8,128)(2,1)}, u32[]{:S(2)}, u32[]{:S(2)}) collective-permute-start(bf16[2,512,1,128]{1,3,2,0:T(8,128)(2,1)} %pad_maximum_fusion.1), channel_id=1, source_target_pairs={{0,32},{16,48},{32,64},{48,80},{64,96},{80,112},{1,33},{17,49},{33... | collective-permute-start | bytes 786440 | tf_op jit(solution)/shard_map/ppermute | solution.py:16
  193.0 4.2 copy-start.2
  197.3 4.0 copy-start.14
  197.3 4.0 copy-start.17
  197.3 4.0 copy-start.19
  207.8 9.7 %copy-start.15 = (bf16[128,2,512]{2,0,1:T(8,128)(2,1)}, bf16[128,2,512]{2,0,1:T(8,128)(2,1)S(1)}, u32[]{:S(2)}) copy-start(bf16[128,2,512]{2,0,1:T(8,128)(2,1)S(1)} %get-tuple-element.26) | copy-start | bytes 786436
  298.5 356.3 %all-reduce.6.cloned.1.call-start = ((), (), s32[]{:S(2)}) async-start(), calls=%async_computation | async-start | bytes 11010048 | tf_op jit(solution)/shard_map/psum | solution.py:291
  302.2 6.4 collective-permute-start.2
  303.5 11.3 %collective-permute-start.3 = (bf16[2,512,1,128]{1,3,2,0:T(8,128)(2,1)}, bf16[2,512,1,128]{1,3,2,0:T(8,128)(2,1)}, u32[]{:S(2)}, u32[]{:S(2)}) collective-permute-start(bf16[2,512,1,128]{1,3,2,0:T(8,128)(2,1)} %get-tuple-element.14), channel_id=1, source_target_pairs={{32,0},{48,16},{64,32},{80,48},{96,64},{112,80},{33,1},{49,17},{65... | collective-permute-start | bytes 786440 | tf_op jit(solution)/shard_map/ppermute | solution.py:16
  316.1 8.2 copy-start.5
  316.9 13.8 %copy-start.23 = (bf16[512,16]{0,1:T(8,128)(2,1)}, bf16[512,16]{0,1:T(8,128)(2,1)S(1)}, u32[]{:S(2)}) copy-start(bf16[512,16]{0,1:T(8,128)(2,1)S(1)} %fusion.66) | copy-start | bytes 49156
  316.9 7.4 copy-start.27
  317.0 7.4 copy-start.33
  317.0 7.9 copy-start.31
  317.0 8.1 copy-start.4
  324.9 5.8 copy-start.21
  324.9 5.8 copy-start.22
  325.0 5.7 copy-start.25
  325.0 5.7 copy-start.12
  330.7 5.7 copy-start.7
  351.0 120.2 %copy-start.6 = (f32[2,512,1,128]{1,3,2,0:T(8,128)S(1)}, f32[2,512,1,128]{1,3,2,0:T(8,128)}, u32[]{:S(2)}) copy-start(f32[2,512,1,128]{1,3,2,0:T(8,128)} %copy-done.5) | copy-start | bytes 1572868
  351.0 567.1 %all-reduce.8.cloned.1.call-start = ((), (), s32[]{:S(2)}) async-start(), calls=%async_computation.1 | async-start | bytes 2064384 | tf_op jit(solution)/shard_map/psum | solution.py:273
  (11 other events, 39.4 us)
Sparse Core Ops, SparseCore 0:
  9.8 90.8 all-gather.4
  102.4 90.5 all-gather.6
  298.6 169.7 all-reduce.9
  471.0 183.8 all-reduce.5
  660.7 257.3 all-reduce.7
where the time goes:
time: 928 us; the launch traced here: 927 us
  waiting for transfers between devices  624 us (67%)
  blocking collectives  166 us (18%)
  matrix products  84.1 us (9%)
  other arithmetic  19 us (2%)
  between operations  14.4 us (2%)
  local copies, waits for them, and re-layouts  10.5 us (1%)
    psum x1, waiting for transfers between devices, local(): grad_down_qkv = lax.psum(grad_down_part, ('dp', 'context', 'tensor'))  262 us
    psum x1, waiting for transfers between devices, local(): lax.psum(output_up_gradient_piece.astype(jnp.bfloat16), ('dp', 'context'))  114 us
    psum x1, blocking collectives, local(): lax.psum(query_up_gradient_piece.astype(jnp.bfloat16), ('dp', 'context'))  90.5 us
    all_gather x1, waiting for transfers between devices, local(): lax.all_gather(tokens[0], 'tensor', axis=0, tiled=True)  86.9 us
    psum x1, waiting for transfers between devices, local(): lax.psum((term + jnp.dot(hidden_all, down_factors_all, preferred_element_...  85.8 us
    psum x1, blocking collectives, local(): factor_value = lax.psum(factor_part.astype(jnp.bfloat16), 'tensor')  75.9 us
    all_gather x1, waiting for transfers between devices, local(): lax.all_gather(output_gradient[0], 'tensor', axis=0, tiled=True)  67.7 us
  transfers between devices with their start and end apart: 9, of which 6 were waited for; matrix products, arithmetic and copies ran while one was open for 10% of the time, Pallas kernels for 0%

commit v1 on v0

--- a/solution.py
+++ b/solution.py
@@ -277,9 +277,9 @@
         ),
         lax.psum(grad_up_kv_part.astype(jnp.bfloat16), ("dp", "context")).astype(jnp.float32),
         lax.psum(grad_down_out_part.astype(jnp.bfloat16), ("dp", "context")).astype(jnp.float32),
-        lax.psum(output_up_gradient_piece.astype(jnp.bfloat16), ("dp", "context")).astype(
-            jnp.float32
-        ),
+        jnp.sum(
+            lax.all_gather(output_up_gradient_piece.astype(jnp.bfloat16), ("dp", "context")), axis=0
+        ).astype(jnp.float32),
     )
     term = jnp.einsum("th,dh->td", query_gradient, query_weight, preferred_element_type=jnp.float32)
     term = term + jnp.einsum(

time: 928 us -> 813 us (0.88)
  waiting for transfers between devices: 624 us -> 507 us
    psum x1 -> x0, waiting for transfers between devices: 114 us -> none  [local(): lax.psum(output_up_gradient_piece.astype(jnp.bfloat16), ('dp', 'context'))]
  transfers between devices with their start and end apart: 9 -> 9, of which waited for: 6 -> 5; matrix products, arithmetic and copies ran while one was open for 10% -> 13% of each run, Pallas kernels for 0% -> 0%
where the time goes in v1:
time: 813 us; the launch traced here: 812 us
  waiting for transfers between devices  507 us (62%)
  blocking collectives  164 us (20%)
  matrix products  86.8 us (11%)
  other arithmetic  18.8 us (2%)
  between operations  14.5 us (2%)
  local copies, waits for them, and re-layouts  11.9 us (1%)
  starting transfers between devices  9.02 us (1%)
    psum x1, waiting for transfers between devices, local(): grad_down_qkv = lax.psum(grad_down_part, ('dp', 'context', 'tensor'))  261 us
    psum x1, blocking collectives, local(): lax.psum(query_up_gradient_piece.astype(jnp.bfloat16), ('dp', 'context'))  88.4 us
    all_gather x1, waiting for transfers between devices, local(): lax.all_gather(tokens[0], 'tensor', axis=0, tiled=True)  86.8 us
    psum x1, waiting for transfers between devices, local(): lax.psum((term + jnp.dot(hidden_all, down_factors_all, preferred_element_...  84.5 us
    psum x1, blocking collectives, local(): factor_value = lax.psum(factor_part.astype(jnp.bfloat16), 'tensor')  75.9 us
    all_gather x1, waiting for transfers between devices, local(): lax.all_gather(output_gradient[0], 'tensor', axis=0, tiled=True)  66.1 us
  transfers between devices with their start and end apart: 9, of which 5 were waited for; matrix products, arithmetic and copies ran while one was open for 13% of the time, Pallas kernels for 0%

profile of v1, /device:TPU:2, one launch (start us, length us, event | category | flops | bytes accessed | tf_op | source)
XLA Modules:
  0.0 812.1 jit_solution(6351807161466027711)
XLA Ops:
  10.3 1.8 multiply_cosine_fusion
  12.1 1.7 fusion.29
  13.8 86.8 %all-gather.7.cloned.1.call-done = bf16[1,512,5376]{2,1,0:T(8,128)(2,1)} async-done(((bf16[1,32,5376]{2,1,0:T(8,128)(2,1)}), bf16[1,512,5376]{2,1,0:T(8,128)(2,1)}) %all-gather.7.cloned.1.call-update) | async-done | bytes 5505040 | tf_op jit(solution)/shard_map/all_gather | solution.py:121
  100.6 4.5 fusion.55
  105.2 3.5 fusion.15
  109.0 2.0 fusion.19
  112.5 2.0 collective-permute-start.1
  114.5 4.0 collective-permute-start
  121.3 1.9 copy.65
  123.3 2.0 copy.64
  125.2 66.1 %all-gather.9.cloned.1.call-done = bf16[1,512,5376]{2,1,0:T(8,128)(2,1)} async-done(((bf16[1,32,5376]{2,1,0:T(8,128)(2,1)}), bf16[1,512,5376]{2,1,0:T(8,128)(2,1)}) %all-gather.9.cloned.1.call-update) | async-done | bytes 5505040 | tf_op jit(solution)/shard_map/all_gather | solution.py:122
  191.4 4.2 fusion.61
  195.7 3.5 fusion.9
  204.2 2.3 fusion.75
  208.1 75.9 %psum.47 = bf16[512,16]{1,0:T(8,128)(2,1)} all-reduce(bf16[512,16]{1,0:T(8,128)(2,1)} %convolution_convert_fusion), channel_id=1, replica_groups=mesh['dp'=2,'context'=8,'tensor'=16] {'tensor'}, use_global_device_ids=true, to_apply=%region_7.8 | all-reduce | flops 8192 | bytes 32768 | tf_op jit(solution)/shard_map/psum | solution.py:269
  284.0 4.2 fusion
  288.3 4.3 fusion.31
  292.6 5.0 fusion.22
  305.4 1.8 copy.40
  308.3 6.5 collective-permute-done.3
  319.7 7.0 fusion.99
  326.7 5.6 fusion.38
  332.3 5.7 fusion.35
  338.0 14.6 %add_convert_fusion = bf16[512,5376]{1,0:T(8,128)(2,1)} fusion(f32[512,5376]{1,0:T(8,128)} %fusion.99, f32[512,5376]{1,0:T(8,128)} %fusion.35, f32[512,5376]{1,0:T(8,128)} %fusion.38, bf16[512,256]{0,1:T(8,128)(2,1)S(1)} %bitcast.199, bf16[5376,256]{1,0:T(8,128)(2,1)S(1)} %copy-done), kind=kOutput, calls=%fused_computation | convolution fusion | flops 1420296192 | bytes 41549824 | tf_op jit(solution)/shard_map/th,dh->td/dot_general | solution.py:284
  352.6 1.8 convolution_convert_fusion.1
  357.8 88.4 %all-reduce.1 = (bf16[16,256]{1,0:T(8,128)(2,1)S(1)}, bf16[2,16,128]{2,1,0:T(8,128)(2,1)S(1)}, bf16[16,256]{1,0:T(8,128)(2,1)S(1)}) all-reduce(bf16[16,256]{1,0:T(8,128)(2,1)} %fusion.67, bf16[2,16,128]{2,1,0:T(8,128)(2,1)S(1)} %pad_maximum_fusion.12, ...), channel_id=1, replica_groups=mesh['dp'=2,'context'=8,'tensor'=16] {'dp','context'}, use_global_device_ids=true, to_apply=%region_4.5 | all-reduce | flops 12288 | bytes 49152 | tf_op jit(solution)/shard_map/psum | solution.py:275
  448.0 4.7 fusion.11
  452.8 2.2 reduce_sum.22
  455.7 84.5 %all-reduce.5.cloned.1.call-done = bf16[512,5376]{1,0:T(8,128)(2,1)} async-done(((bf16[512,5376]{1,0:T(8,128)(2,1)}), bf16[512,5376]{1,0:T(8,128)(2,1)}) %all-reduce.5.cloned.1.call-update) | async-done | bytes 5505040 | tf_op jit(solution)/shard_map/psum | solution.py:291
  540.2 1.7 fusion.77
  541.9 261.4 %all-reduce.7.cloned.1.call-done = f32[3,16,5376]{2,1,0:T(8,128)} async-done(((f32[3,16,5376]{2,1,0:T(8,128)}), f32[3,16,5376]{2,1,0:T(8,128)}) %all-reduce.7.cloned.1.call-update) | async-done | bytes 1032208 | tf_op jit(solution)/shard_map/psum | solution.py:273
  803.3 2.2 copy.68
  (139 shorter events, 33.8 us)
Async XLA Ops:
  7.2 111.4 %copy-start = (bf16[5376,256]{1,0:T(8,128)(2,1)S(1)}, bf16[5376,256]{1,0:T(8,128)(2,1)}, u32[]{:S(2)}) copy-start(bf16[5376,256]{1,0:T(8,128)(2,1)} %param.14) | copy-start | bytes 8257540
  7.2 93.5 %all-gather.7.cloned.1.call-start = ((), (), s32[]{:S(2)}) async-start(), calls=%async_computation.2 | async-start | bytes 5849088 | tf_op jit(solution)/shard_map/all_gather | solution.py:121
  7.9 183.5 %all-gather.9.cloned.1.call-start = ((), (), s32[]{:S(2)}) async-start(), calls=%async_computation.3 | async-start | bytes 5849088 | tf_op jit(solution)/shard_map/all_gather | solution.py:122
  8.7 444.1 %all-gather.11.cloned.1.call-start = ((), (), s32[]{:S(2)}) async-start(), calls=%async_computation.4 | async-start | bytes 2924544 | tf_op jit(solution)/shard_map/all_gather | solution.py:281
  8.7 102.4 %copy-start.41 = (f32[64]{0:T(128)}, f32[64]{0:T(128)S(1)}, u32[]{:S(2)}) copy-start(f32[64]{0:T(128)S(1)} %negate_power_fusion) | copy-start | bytes 772
  8.8 102.4 %copy-start.37 = (f32[512]{0:T(512)}, f32[512]{0:T(512)S(1)}, u32[]{:S(2)}) copy-start(f32[512]{0:T(512)S(1)} %fusion.114) | copy-start | bytes 6148
  100.6 4.5 copy-start.1
  105.2 15.0 %copy-start.29 = (bf16[512,48]{0,1:T(8,128)(2,1)}, bf16[512,48]{0,1:T(8,128)(2,1)S(1)}, u32[]{:S(2)}) copy-start(bf16[512,48]{0,1:T(8,128)(2,1)S(1)} %fusion.55) | copy-start | bytes 147460
  111.2 9.1 %copy-start.39 = (bf16[16,256]{1,0:T(8,128)(2,1)S(1)}, bf16[16,256]{1,0:T(8,128)(2,1)}, u32[]{:S(2)}) copy-start(bf16[16,256]{1,0:T(8,128)(2,1)} %param.18) | copy-start | bytes 24580
  112.5 87.2 %collective-permute-start.1 = (bf16[2,512,1,128]{1,3,2,0:T(8,128)(2,1)}, bf16[2,512,1,128]{1,3,2,0:T(8,128)(2,1)}, u32[]{:S(2)}, u32[]{:S(2)}) collective-permute-start(bf16[2,512,1,128]{1,3,2,0:T(8,128)(2,1)} %pad_maximum_fusion.1), channel_id=1, source_target_pairs={{0,16},{16,32},{32,48},{48,64},{64,80},{80,96},{96,112},{1,17},{17... | collective-permute-start | bytes 786440 | tf_op jit(solution)/shard_map/ppermute | solution.py:16
  114.5 85.2 %collective-permute-start = (bf16[2,512,1,128]{1,3,2,0:T(8,128)(2,1)}, bf16[2,512,1,128]{1,3,2,0:T(8,128)(2,1)}, u32[]{:S(2)}, u32[]{:S(2)}) collective-permute-start(bf16[2,512,1,128]{1,3,2,0:T(8,128)(2,1)} %pad_maximum_fusion.1), channel_id=1, source_target_pairs={{0,32},{16,48},{32,64},{48,80},{64,96},{80,112},{1,33},{17,49},{33... | collective-permute-start | bytes 786440 | tf_op jit(solution)/shard_map/ppermute | solution.py:16
  191.4 4.2 copy-start.2
  195.7 4.1 copy-start.19
  195.7 4.1 copy-start.26
  199.5 4.7 copy-start.32
  288.2 251.9 %all-reduce.5.cloned.1.call-start = ((), (), s32[]{:S(2)}) async-start(), calls=%async_computation | async-start | bytes 11010048 | tf_op jit(solution)/shard_map/psum | solution.py:291
  288.3 4.3 copy-start.17
  288.3 4.3 copy-start.33
  292.6 6.5 copy-start.9
  292.6 5.0 copy-start.22
  292.6 5.0 copy-start.24
  297.6 6.6 copy-start.11
  297.6 6.6 copy-start.13
  300.0 8.3 %collective-permute-start.2 = (bf16[2,512,1,128]{1,3,2,0:T(8,128)(2,1)}, bf16[2,512,1,128]{1,3,2,0:T(8,128)(2,1)}, u32[]{:S(2)}, u32[]{:S(2)}) collective-permute-start(bf16[2,512,1,128]{1,3,2,0:T(8,128)(2,1)} %get-tuple-element.13), channel_id=1, source_target_pairs={{16,0},{32,16},{48,32},{64,48},{80,64},{96,80},{112,96},{17,1},{33... | collective-permute-start | bytes 786440 | tf_op jit(solution)/shard_map/ppermute | solution.py:16
  301.3 13.5 %collective-permute-start.3 = (bf16[2,512,1,128]{1,3,2,0:T(8,128)(2,1)}, bf16[2,512,1,128]{1,3,2,0:T(8,128)(2,1)}, u32[]{:S(2)}, u32[]{:S(2)}) collective-permute-start(bf16[2,512,1,128]{1,3,2,0:T(8,128)(2,1)} %get-tuple-element.14), channel_id=1, source_target_pairs={{32,0},{48,16},{64,32},{80,48},{96,64},{112,80},{33,1},{49,17},{65... | collective-permute-start | bytes 786440 | tf_op jit(solution)/shard_map/ppermute | solution.py:16
  316.0 16.4 %copy-start.6 = (f32[2,512,1,128]{1,3,2,0:T(8,128)}, f32[2,512,1,128]{1,3,2,0:T(8,128)S(1)}, u32[]{:S(2)}) copy-start(f32[2,512,1,128]{1,3,2,0:T(8,128)S(1)} %fusion.74) | copy-start | bytes 1572868
  317.3 9.3 %copy-start.30 = (bf16[512,1,64]{0,2,1:T(8,128)(2,1)}, bf16[512,1,64]{0,2,1:T(8,128)(2,1)S(1)}, u32[]{:S(2)}) copy-start(bf16[512,1,64]{0,2,1:T(8,128)(2,1)S(1)} %get-tuple-element.17) | copy-start | bytes 196612
  317.4 9.3 %copy-start.31 = (bf16[512,1,64]{0,2,1:T(8,128)(2,1)}, bf16[512,1,64]{0,2,1:T(8,128)(2,1)S(1)}, u32[]{:S(2)}) copy-start(bf16[512,1,64]{0,2,1:T(8,128)(2,1)S(1)} %get-tuple-element.18) | copy-start | bytes 196612
  319.7 7.0 copy-start.4
  332.3 5.7 copy-start.8
  352.6 4.4 copy-start.7
  352.6 450.8 %all-reduce.7.cloned.1.call-start = ((), (), s32[]{:S(2)}) async-start(), calls=%async_computation.1 | async-start | bytes 2064384 | tf_op jit(solution)/shard_map/psum | solution.py:273
  (19 other events, 56.9 us)
Sparse Core Ops, SparseCore 0:
  9.8 90.8 all-gather.6
  102.4 88.9 all-gather.8
  288.4 69.6 all-gather.10
  360.5 179.5 all-reduce.4
  546.1 257.2 all-reduce.6
